TPU v7x, 128 devices: a whole 4x4x4 slice. The times are simulated.
128 devices in a mesh: cells: 128 (over x, z, y, core).
Axes of the slice: x: 4, y: 4, z: 4, core: 2. Of those that a mesh axis runs over, the one named last changes fastest.
Arguments:
- src_feat: bfloat16 [2048, 32, 256], P('cells'), may hold values from -16 to 16
- tgt_feat: bfloat16 [2048, 32, 256], P('cells'), may hold values from -16 to 16
- src_len: int32 [2048], P('cells'), may hold values from 64 to 256, as said below
- tgt_len: int32 [2048], P('cells'), may hold values from 64 to 256, as said below
- neighbours: int32 [2048, 5], P('cells'), may hold values from 0 to 2047, as said below
Outputs:
- source_pot: float32 [2048, 256], P('cells')
- target_pot: float32 [2048, 256], P('cells')
Inputs may be any that keep to these rules, and one draw needn't show every extreme that they name: `src_len`: some cell holds 256 live points. `tgt_len`: some cell holds 256 live points. `neighbours`: cell c lies on device c // 16. The five cells of a row lie on five different devices, none of them the row's own. Of all entries in the rows of one device, at most 1 name cells of any one device, and in every draw some device has 1 entries naming one device.
All inputs are finite; a program needn't handle non-finite values.
Results may differ from a plain program's by a relative error of at most 0.0005.
Values may be sent and summed in bfloat16 or wider, within the bound.
A program may use at most 64 MiB of HBM per device.

v0:
```python
import jax
import jax.numpy as jnp
from jax import lax
from jax.sharding import Mesh
from jax.sharding import PartitionSpec as P

ITERS = 2
CELLS = ("cells_0", "cells_1", "cells_2", "cells_3")


entropy_scale = 0.5
marginal_weight = 1.0
damping = marginal_weight / (marginal_weight + entropy_scale)
masked_score = -1e30


def laid_out(parts, dim):
    parts = jnp.moveaxis(parts, 0, dim)
    lengths = parts.shape
    return parts.reshape(*lengths[:dim], lengths[dim] * lengths[dim + 1], *lengths[dim + 2 :])


def all_blocks(array, axes, sequence):
    parts = array[None]
    for k in sequence:
        parts = lax.all_gather(parts, axes[k], axis=0, tiled=True)
    held = [lax.axis_size(axes[k]) for k in reversed(sequence)]
    parts = parts.reshape(*held, *array.shape)
    turned = sorted(range(len(sequence)), key=lambda place: sequence[len(sequence) - 1 - place])
    return parts.transpose(*turned, *range(len(sequence), parts.ndim)).reshape(-1, *array.shape)


def gather_axes(array, axes, sequence, dim):
    return laid_out(all_blocks(array, axes, sequence), dim)


def side_by_side(arrays, axis, split_dim, concat_dim, along):
    ends, at = ([], 0)
    for a in arrays[:-1]:
        at += a.shape[along]
        ends.append(at)
    both = jnp.concatenate(arrays, axis=along)
    return tuple(
        jnp.split(
            lax.all_to_all(both, axis, split_axis=split_dim, concat_axis=concat_dim, tiled=True),
            ends,
            axis=along,
        )
    )


def live_points(lengths, points):
    return lax.broadcasted_iota(jnp.int32, (lengths.shape[0], points), 1) < lengths[:, None]


def half_norms(features):
    widened = features.astype(jnp.float32)
    return 0.5 * jnp.sum(widened * widened, axis=-2)


def pair_costs(source_block, source_norm, target_block, target_norm):
    cross = jnp.einsum(
        "gfp,gkfq->gpkq", source_block, target_block, preferred_element_type=jnp.float32
    )
    return source_norm[:, :, None, None] + target_norm[:, None, :, :] - cross


def target_scores(
    source_block, norm_block, source_mask, source_values, target_block, target_norm_block
):
    pair_cost = pair_costs(source_block, norm_block, target_block, target_norm_block)
    scores = jnp.where(
        source_mask[:, :, None, None],
        (source_values[:, :, None, None] - pair_cost) / entropy_scale,
        masked_score,
    )
    peak_score = jnp.max(scores, axis=1)
    totals = jnp.sum(jnp.exp(scores - peak_score[:, None]), axis=1)
    return (peak_score, totals)


def in_groups(function, arrays, group_size):
    shaped = tuple(
        (
            item.reshape((item.shape[0] // group_size, group_size) + item.shape[1:])
            for item in arrays
        )
    )
    result = lax.map(lambda items: function(*items), shaped)
    return jax.tree.map(
        lambda piece: piece.reshape((piece.shape[0] * piece.shape[1],) + piece.shape[2:]), result
    )


def local(src_feat, tgt_feat, src_len, tgt_len, neighbours):
    cells_here, channels, points = src_feat.shape
    devices = lax.axis_size(CELLS)
    per_owner = (5 * cells_here + devices - 2) // (devices - 1)
    slot_count = devices * per_owner
    group_size = max(1, cells_here // 16)
    src_live = live_points(src_len, points)
    tgt_live = live_points(tgt_len, points)
    all_lengths = gather_axes(tgt_len, (("cells_0", "cells_1", "cells_2"), "cells_3"), (0, 1), 0)
    wanted = neighbours.reshape(-1)
    entries = wanted.shape[0]
    owners = wanted // cells_here
    local_cell = wanted % cells_here
    earlier = lax.broadcasted_iota(jnp.int32, (entries, entries), 1) < lax.broadcasted_iota(
        jnp.int32, (entries, entries), 0
    )
    ranking = jnp.sum(((owners[:, None] == owners[None, :]) & earlier).astype(jnp.int32), axis=1)
    slot_of = owners * per_owner + ranking
    placed = slot_of[:, None] == jnp.arange(slot_count, dtype=jnp.int32)[None, :]
    outgoing = jnp.max(jnp.where(placed, local_cell[:, None], -1), axis=0)
    incoming = lax.all_to_all(
        outgoing.reshape(devices, per_owner), CELLS, split_axis=0, concat_axis=0, tiled=True
    )
    incoming_ids = incoming.reshape(-1)
    served = jnp.maximum(incoming_ids, 0)
    filled = incoming_ids >= 0
    sending_blocks = jnp.take(tgt_feat, served, axis=0).reshape(
        devices, per_owner, channels, points
    )
    arrived_blocks = lax.all_to_all(
        sending_blocks, CELLS, split_axis=0, concat_axis=0, tiled=True
    ).reshape(slot_count, channels, points)
    remote = jnp.take(arrived_blocks, slot_of, axis=0).reshape(cells_here, 5, channels, points)
    target_blocks = jnp.concatenate([tgt_feat[:, None], remote], axis=1)
    target_norm = half_norms(target_blocks)
    remote_live = live_points(jnp.take(all_lengths, wanted), points).reshape(cells_here, 5, points)
    block_live = jnp.concatenate([tgt_live[:, None], remote_live], axis=1)
    source_norm = half_norms(src_feat)
    cell_ids = jnp.arange(cells_here, dtype=jnp.int32)
    member = (cell_ids[:, None] == incoming_ids[None, :]).astype(jnp.float32)
    target_pot = jnp.zeros((cells_here, points), jnp.float32)
    source_pot = jnp.zeros((cells_here, points), jnp.float32)
    for iteration in range(ITERS):
        if iteration == 0:
            remote_pot = jnp.zeros((cells_here, 5, points), jnp.float32)
        else:
            sending = jnp.take(target_pot, served, axis=0).reshape(devices, per_owner, points)
            arrived = (
                lax.all_to_all(
                    sending.astype(jnp.bfloat16), CELLS, split_axis=0, concat_axis=0, tiled=True
                )
                .astype(sending.dtype)
                .reshape(slot_count, points)
            )
            remote_pot = jnp.take(arrived, slot_of, axis=0).reshape(cells_here, 5, points)
        potential_blocks = jnp.concatenate([target_pot[:, None], remote_pot], axis=1)

        def per_group(
            source_block,
            norm_block,
            source_mask,
            target_block,
            target_norm_block,
            potential_block,
            target_mask,
        ):
            pair_cost = pair_costs(source_block, norm_block, target_block, target_norm_block)
            scores = jnp.where(
                target_mask[:, None, :, :],
                (potential_block[:, None, :, :] - pair_cost) / entropy_scale,
                masked_score,
            )
            peak_score = jnp.max(scores, axis=(2, 3))
            totals = jnp.sum(jnp.exp(scores - peak_score[:, :, None, None]), axis=(2, 3))
            return jnp.where(
                source_mask, -damping * entropy_scale * (peak_score + jnp.log(totals)), 0.0
            )

        source_pot = in_groups(
            per_group,
            (
                src_feat,
                source_norm,
                src_live,
                target_blocks,
                target_norm,
                potential_blocks,
                block_live,
            ),
            group_size,
        )
        peaks, sums = in_groups(
            target_scores,
            (src_feat, source_norm, src_live, source_pot, target_blocks, target_norm),
            group_size,
        )
        send_peaks = (
            jnp.zeros((slot_count, points), jnp.float32)
            .at[slot_of]
            .set(peaks[:, 1:].reshape(-1, points))
        )
        send_sums = (
            jnp.zeros((slot_count, points), jnp.float32)
            .at[slot_of]
            .set(sums[:, 1:].reshape(-1, points))
        )
        got_peaks, got_sums = side_by_side(
            (
                send_peaks.reshape(devices, per_owner, points),
                send_sums.reshape(devices, per_owner, points),
            ),
            CELLS,
            0,
            0,
            1,
        )
        got_peaks = got_peaks.reshape(slot_count, points)
        got_sums = got_sums.reshape(slot_count, points)

        def largest_of(cell_group, own_peaks):
            hits = incoming_ids[:, None] == cell_group[None, :]
            candidate = jnp.max(
                jnp.where(hits[:, :, None], got_peaks[:, None, :], masked_score), axis=0
            )
            return jnp.maximum(candidate, own_peaks)

        largest = in_groups(largest_of, (cell_ids, peaks[:, 0]), group_size)
        weighted = jnp.where(
            filled[:, None], got_sums * jnp.exp(got_peaks - jnp.take(largest, served, axis=0)), 0.0
        )
        update_totals = sums[:, 0] * jnp.exp(peaks[:, 0] - largest) + jnp.dot(
            member, weighted, precision=lax.Precision.HIGHEST, preferred_element_type=jnp.float32
        )
        target_pot = jnp.where(
            tgt_live, -damping * entropy_scale * (largest + jnp.log(update_totals)), 0.0
        )
    return (source_pot, target_pot)


def solution(mesh):
    split = Mesh(mesh.devices.reshape(4, 4, 4, 2), ("cells_0", "cells_1", "cells_2", "cells_3"))
    return jax.shard_map(
        local,
        mesh=split,
        in_specs=(P(CELLS, None, None), P(CELLS, None, None), P(CELLS), P(CELLS), P(CELLS, None)),
        out_specs=(P(CELLS, None), P(CELLS, None)),
        check_vma=False,
    )
```

profile of v0, /device:TPU:1, one launch (start us, length us, event | category | flops | bytes accessed | tf_op | source)
XLA Modules:
  0.0 261.0 jit_solution(9343312779750902399)
XLA Ops:
  0.6 0.8 copy.113
  2.0 20.8 %all_to_all.35 = s32[128,1,1]{2,1,0:T(1,128)S(1)} all-to-all(s32[128,1,1]{2,1,0:T(1,128)S(1)} %copy.120), channel_id=1, replica_groups=mesh['cells_0'=4,'cells_1'=4,'cells_2'=4,'cells_3'=2] {'cells_0','cells_..., dimensions={0} | all-to-all | bytes 1024 | tf_op jit(solution)/shard_map/all_to_all | solution.py:115
  22.8 2.3 reduce.20
  25.9 1.6 bitcast_select_fusion
  27.5 4.6 %all-to-all-start.1 = ((bf16[128,1,32,256]{3,2,1,0:T(8,128)(2,1)}), bf16[128,1,32,256]{3,2,1,0:T(8,128)(2,1)S(1)}, u32[]{:S(2)}, u32[]{:S(2)}) async-start(bf16[128,1,32,256]{3,2,1,0:T(8,128)(2,1)} %bitcast_select_fusion), calls=%async_computation.1 | async-start | bytes 4194304 | tf_op jit(solution)/shard_map/all_to_all | solution.py:124
  33.8 37.3 %all-reduce = s32[1024]{0:T(1024)S(1)} all-reduce(s32[1024]{0:T(1024)S(1)} %dynamic-update-slice), channel_id=2, replica_groups=mesh['cells_0'=4,'cells_1'=4,'cells_2'=4,'cells_3'=2] {'cells_0','cells_..., use_global_device_ids=true, to_apply=%add | all-reduce | flops 1024 | bytes 8192
  71.2 6.5 %all-gather.1 = s32[2,64,16]{1,2,0:T(8,128)S(1)} all-gather(s32[1,64,16]{1,2,0:T(8,128)S(1)} %copy.116), channel_id=1, replica_groups=mesh['cells_0'=4,'cells_1'=4,'cells_2'=4,'cells_3'=2] {'cells_3'}, dimensions={0}, use_global_device_ids=true | all-gather | bytes 12288 | tf_op jit(solution)/shard_map/all_gather | solution.py:26
  78.0 1.1 gather_fusion
  79.7 1.8 gather_fusion.2
  81.6 1.5 broadcast_select_fusion.2
  83.9 16.2 %while.64 = (s32[]{:T(128)}, f32[16,1,256]{2,1,0:T(1,128)S(1)}, pred[16,1,256]{2,1,0:T(4,128)(4,1)S(1)}, pred[16,1,6,256]{3,2,1,0:T(8,128)(4,1)S(1)}, f32[16,1,2...) while((s32[]{:T(128)}, f32[16,1,256]{2,1,0:T(1,128)S(1)}, ...), condition=%wide.region_7.8_spmd, body=%wide.region_4.7_spmd.sunk | while | flops 28311808 | bytes 3299437 | solution.py:89
  100.2 16.5 %while.65 = (s32[]{:T(128)}, f32[16,1,6,256]{3,0,2,1:T(8,128)S(1)}, f32[16,1,6,256]{3,0,2,1:T(8,128)S(1)}, pred[16,1,256]{2,1,0:T(4,128)(4,1)S(1)}, f32[16,1,256...) while((s32[]{:T(128)}, f32[16,1,6,256]{3,0,2,1:T(8,128)S(1)}, ...), condition=%wide.region_11.12_spmd, body=%wide.region_8.11_spmd.sunk | while | flops 28308480 | bytes 3356801 | solution.py:89
  116.9 0.9 scatter_custom_fusion
  117.8 0.9 scatter_custom_fusion.1
  118.7 0.9 copy.128
  119.6 3.8 %all-to-all-start.2 = ((f32[128,2,256]{2,1,0:T(2,128)}), f32[128,2,256]{2,1,0:T(2,128)S(1)}, u32[]{:S(2)}, u32[]{:S(2)}) async-start(f32[128,2,256]{2,1,0:T(2,128)} %copy.128), calls=%async_computation.2 | async-start | bytes 524288 | tf_op jit(solution)/shard_map/all_to_all | solution.py:45
  123.4 10.9 %all-to-all-done.2 = f32[128,2,256]{2,1,0:T(2,128)S(1)} async-done(((f32[128,2,256]{2,1,0:T(2,128)}), f32[128,2,256]{2,1,0:T(2,128)S(1)}, u32[]{:S(2)}, u32[]{:S(2)}) %all-to-all-start.2) | async-done | bytes 262176 | tf_op jit(solution)/shard_map/all_to_all | solution.py:45
  134.5 24.6 %while.66 = (s32[]{:T(128)}, f32[16,1,256]{2,0,1:T(8,128)S(1)}, s32[16,1]{0,1:T(1,128)S(1)}, s32[128,1]{0,1:T(1,128)S(1)}, f32[128,1,256]{2,1,0:T(1,128)S(1)}, /...) while((s32[]{:T(128)}, f32[16,1,256]{2,0,1:T(8,128)S(1)}, s32[16,1]{0,1:T(1,128)S(1)}, ...), condition=%wide.region_16.17_spmd, body=%wide.region_14.16_spmd.sunk | while | flops 65666 | bytes 138093 | solution.py:89
  159.2 0.8 gather_fusion.4
  160.2 0.8 gather_fusion.5
  162.9 4.7 %all-to-all-start.3 = ((bf16[128,2,128]{2,1,0:T(2,128)(2,1)}), bf16[128,2,128]{2,1,0:T(2,128)(2,1)S(1)}, u32[]{:S(2)}, u32[]{:S(2)}) async-start(bf16[128,2,128]{2,1,0:T(2,128)(2,1)} %reshape.884), calls=%async_computation.3 | async-start | bytes 131072 | tf_op jit(solution)/shard_map/all_to_all | solution.py:143
  167.6 9.5 %all-to-all-done.3 = bf16[128,2,128]{2,1,0:T(2,128)(2,1)S(1)} async-done(((bf16[128,2,128]{2,1,0:T(2,128)(2,1)}), bf16[128,2,128]{2,1,0:T(2,128)(2,1)S(1)}, u32[]{:S(2)}, u32[]{:S(2)}) %all-to-all-start.3) | async-done | bytes 65568 | tf_op jit(solution)/shard_map/all_to_all | solution.py:143
  178.0 19.5 %while.67 = (s32[]{:T(128)}, f32[16,1,256]{2,1,0:T(1,128)S(1)}, pred[16,1,256]{2,1,0:T(4,128)(4,1)S(1)}, pred[16,1,6,256]{3,2,1,0:T(8,128)(4,1)S(1)}, f32[16,1,6...) while((s32[]{:T(128)}, f32[16,1,256]{2,1,0:T(1,128)S(1)}, ...), condition=%wide.region_20.22_spmd, body=%wide.region_17.21_spmd.sunk | while | flops 28311808 | bytes 3319925 | solution.py:89
  178.1 0.8 fusion.98
  179.3 0.8 fusion.98
  180.5 0.8 fusion.98
  181.8 0.8 fusion.98
  183.0 0.8 fusion.98
  184.2 0.8 fusion.98
  185.4 0.8 fusion.98
  186.6 0.8 fusion.98
  187.8 0.8 fusion.98
  189.1 0.8 fusion.98
  190.3 0.8 fusion.98
  191.5 0.8 fusion.98
  192.7 0.8 fusion.98
  193.9 0.8 fusion.98
  195.1 0.8 fusion.98
  196.4 0.8 fusion.98
  197.5 16.5 %while.68 = (s32[]{:T(128)}, f32[16,1,6,256]{3,0,2,1:T(8,128)S(1)}, f32[16,1,6,256]{3,0,2,1:T(8,128)S(1)}, pred[16,1,256]{2,1,0:T(4,128)(4,1)S(1)}, f32[16,1,256...) while((s32[]{:T(128)}, f32[16,1,6,256]{3,0,2,1:T(8,128)S(1)}, ...), condition=%wide.region_24.26_spmd, body=%wide.region_21.25_spmd.sunk | while | flops 28308480 | bytes 3356801 | solution.py:89
  214.2 0.9 scatter_custom_fusion.2
  215.1 0.9 scatter_custom_fusion.3
  216.1 0.9 copy.141
  217.0 4.7 %all-to-all-start.4 = ((f32[128,2,256]{2,1,0:T(2,128)}), f32[128,2,256]{2,1,0:T(2,128)S(1)}, u32[]{:S(2)}, u32[]{:S(2)}) async-start(f32[128,2,256]{2,1,0:T(2,128)} %copy.141), calls=%async_computation.4 | async-start | bytes 524288 | tf_op jit(solution)/shard_map/all_to_all | solution.py:45
  222.3 10.2 %all-to-all-done.4 = f32[128,2,256]{2,1,0:T(2,128)S(1)} async-done(((f32[128,2,256]{2,1,0:T(2,128)}), f32[128,2,256]{2,1,0:T(2,128)S(1)}, u32[]{:S(2)}, u32[]{:S(2)}) %all-to-all-start.4) | async-done | bytes 262176 | tf_op jit(solution)/shard_map/all_to_all | solution.py:45
  232.7 26.6 %while.69 = (s32[]{:T(128)}, f32[16,1,256]{2,0,1:T(8,128)S(1)}, s32[16,1]{0,1:T(1,128)S(1)}, s32[128,1]{0,1:T(1,128)S(1)}, f32[128,1,256]{2,1,0:T(1,128)S(1)}, /...) while((s32[]{:T(128)}, f32[16,1,256]{2,0,1:T(8,128)S(1)}, s32[16,1]{0,1:T(1,128)S(1)}, ...), condition=%wide.region_29.31_spmd, body=%wide.region_27.30_spmd.sunk | while | flops 65666 | bytes 138093 | solution.py:89
  259.3 0.8 gather_fusion.6
  260.1 0.9 fusion.27
  (745 shorter events, 110.1 us)
Async XLA Ops:
  0.6 24.5 %copy-start = (bf16[16,32,256]{2,1,0:T(8,128)(2,1)S(1)}, bf16[16,32,256]{2,1,0:T(8,128)(2,1)}, u32[]{:S(2)}) copy-start(bf16[16,32,256]{2,1,0:T(8,128)(2,1)} %param.20) | copy-start | bytes 786436
  27.5 4.8 %copy-start.4 = (u32[128]{0:T(128)S(1)}, u32[128]{0:T(128)}, u32[]{:S(2)}) copy-start(u32[128]{0:T(128)} %constant.244) | copy-start | bytes 1540
  27.5 6.1 %copy-start.2 = (s32[16]{0:T(128)S(1)}, s32[16]{0:T(128)}, u32[]{:S(2)}) copy-start(s32[16]{0:T(128)} %param.22) | copy-start | bytes 196
  27.5 51.7 %copy-start.1 = (bf16[16,32,256]{2,1,0:T(8,128)(2,1)S(1)}, bf16[16,32,256]{2,1,0:T(8,128)(2,1)}, u32[]{:S(2)}) copy-start(bf16[16,32,256]{2,1,0:T(8,128)(2,1)} %param.19) | copy-start | bytes 786436
  27.5 52.1 %copy-start.3 = (s32[16]{0:T(128)S(1)}, s32[16]{0:T(128)}, u32[]{:S(2)}) copy-start(s32[16]{0:T(128)} %param.21) | copy-start | bytes 196
  27.5 52.2 %all-to-all-start.1 = ((bf16[128,1,32,256]{3,2,1,0:T(8,128)(2,1)}), bf16[128,1,32,256]{3,2,1,0:T(8,128)(2,1)S(1)}, u32[]{:S(2)}, u32[]{:S(2)}) async-start(bf16[128,1,32,256]{3,2,1,0:T(8,128)(2,1)} %bitcast_select_fusion), calls=%async_computation.1 | async-start | bytes 4194304 | tf_op jit(solution)/shard_map/all_to_all | solution.py:124
  119.6 14.7 %all-to-all-start.2 = ((f32[128,2,256]{2,1,0:T(2,128)}), f32[128,2,256]{2,1,0:T(2,128)S(1)}, u32[]{:S(2)}, u32[]{:S(2)}) async-start(f32[128,2,256]{2,1,0:T(2,128)} %copy.128), calls=%async_computation.2 | async-start | bytes 524288 | tf_op jit(solution)/shard_map/all_to_all | solution.py:45
  162.9 14.3 %all-to-all-start.3 = ((bf16[128,2,128]{2,1,0:T(2,128)(2,1)}), bf16[128,2,128]{2,1,0:T(2,128)(2,1)S(1)}, u32[]{:S(2)}, u32[]{:S(2)}) async-start(bf16[128,2,128]{2,1,0:T(2,128)(2,1)} %reshape.884), calls=%async_computation.3 | async-start | bytes 131072 | tf_op jit(solution)/shard_map/all_to_all | solution.py:143
  217.0 15.5 %all-to-all-start.4 = ((f32[128,2,256]{2,1,0:T(2,128)}), f32[128,2,256]{2,1,0:T(2,128)S(1)}, u32[]{:S(2)}, u32[]{:S(2)}) async-start(f32[128,2,256]{2,1,0:T(2,128)} %copy.141), calls=%async_computation.4 | async-start | bytes 524288 | tf_op jit(solution)/shard_map/all_to_all | solution.py:45
where the time goes:
time: 262 us; the launch traced here: 261 us
  blocking collectives  64.6 us (25%)
  other arithmetic  54.1 us (21%)
  local copies, waits for them, and re-layouts  45.8 us (17%)
  matrix products  41.3 us (16%)
  waiting for transfers between devices  30.6 us (12%)
  starting transfers between devices  17.8 us (7%)
  loops' own time  5 us (2%)
    dot_general x64, matrix products, pair_costs(): jnp.einsum('gfp,gkfq->gpkq', source_block, target_block, preferred_elemen...  40.1 us
    unnamed x1, blocking collectives  37.3 us
    dynamic_slice x128, local copies, waits for them, and re-layouts, in_groups(): result = lax.map(lambda items: function(*items), shaped)  21.5 us
    eq x32, other arithmetic, largest_of(): hits = incoming_ids[:, None] == cell_group[None, :]  21.5 us
    all_to_all x2, waiting for transfers between devices, side_by_side(): lax.all_to_all(both, axis, split_axis=split_dim, concat_axis=concat_dim,...  21.1 us
    all_to_all x1, blocking collectives, local(): lax.all_to_all(outgoing.reshape(devices, per_owner), CELLS, split_axis=0,...  20.8 us
    all_to_all x1, waiting for transfers between devices, local(): lax.all_to_all(sending.astype(jnp.bfloat16), CELLS, split_axis=0, concat_...  9.5 us
    reduce_sum x32, other arithmetic, per_group(): jnp.sum(jnp.exp(scores - peak_score[:, :, None, None]), axis=(2, 3))  9.41 us
  transfers between devices with their start and end apart: 4, of which 3 were waited for; matrix products, arithmetic and copies ran while one was open for 1% of the time, Pallas kernels for 0%

commit v1 on v0

v1 whole, which is shorter than its diff:
```python
import functools
import math

import jax
import jax.numpy as jnp
from jax import lax
from jax.experimental import pallas as pl
from jax.experimental.pallas import tpu as pltpu
from jax.sharding import PartitionSpec as P

MESH = pl.DeviceIdType.MESH
ITERS = 2
LIST = 6
entropy_scale = 0.5
marginal_weight = 1.0
damping = marginal_weight / (marginal_weight + entropy_scale)
UNIT = math.log2(math.e) / entropy_scale
NEVER = -1.0e30
FAR = 2.0**50
AUX = 16


def peer_of(me, k):
    core, y, z, x = me % 2, (me // 2) % 4, (me // 8) % 4, me // 32
    dcore, dy, dz, dx = k % 2, (k // 2) % 4, (k // 8) % 4, k // 32
    return ((((x + dx) % 4) * 4 + (z + dz) % 4) * 4 + (y + dy) % 4) * 2 + (core + dcore) % 2


def three_parts(value):
    high = value.astype(jnp.bfloat16).astype(jnp.float32)
    rest = value - high
    middle = rest.astype(jnp.bfloat16).astype(jnp.float32)
    return high, middle, rest - middle


def aux_rows(first, value, points):
    row = lax.broadcasted_iota(jnp.int32, (AUX, points), 0)
    rows = jnp.where(row < 6, 1.0, 0.0)
    for i, piece in enumerate(three_parts(value)):
        rows = jnp.where(row == first + i, piece, rows)
    return rows.astype(jnp.bfloat16)


def cross(a, b):
    return lax.dot_general(a, b, (((0,), (0,)), ((), ())), preferred_element_type=jnp.float32)


def kernel(
    n,
    src,
    tgt,
    src_len,
    tgt_len,
    near,
    entry_of,
    asked,
    source_out,
    target_out,
    masked,
    heard,
    row_ids,
    ids,
    send_feat,
    got_feat,
    xaug,
    xnorm,
    yaug,
    ynorm,
    scores,
    part,
    pots,
    send_part,
    got_part,
    send_pot,
    got_pot,
    send_sems,
    recv_sems,
    local_sem,
):
    cells, channels, points = src.shape
    me = lax.axis_index("cells")
    lanes = lax.broadcasted_iota(jnp.int32, (1, points), 1)
    cell_row = lax.broadcasted_iota(jnp.int32, (cells, points), 0)
    top = 3 * channels

    barrier = pltpu.get_barrier_semaphore()

    def greet(k, _):
        pl.semaphore_signal(barrier, inc=1, device_id=(peer_of(me, k),), device_id_type=MESH)
        return 0

    lax.fori_loop(1, n, greet, 0)

    def prepare(c, _):
        live = lanes < tgt_len[c]
        masked[c] = jnp.where(live, tgt[c].astype(jnp.float32), FAR).astype(jnp.bfloat16)
        x = src[c].astype(jnp.float32)
        for i, piece in enumerate(three_parts(x * UNIT)):
            xaug[c, i * channels : (i + 1) * channels] = piece.astype(jnp.bfloat16)
        norm = (-0.5 * UNIT) * jnp.sum(x * x, axis=0, keepdims=True)
        xnorm[c] = norm
        xaug[c, top : top + AUX] = aux_rows(0, norm, points)
        return 0

    lax.fori_loop(0, cells, prepare, 0)
    pl.semaphore_wait(barrier, n - 1)

    def send(outgoing, incoming, sem):
        def go(k, _):
            peer = peer_of(me, k)
            pltpu.make_async_remote_copy(
                src_ref=outgoing.at[peer],
                dst_ref=incoming.at[me],
                send_sem=send_sems.at[sem],
                recv_sem=recv_sems.at[sem],
                device_id=(peer,),
                device_id_type=MESH,
            ).start()
            return 0

        lax.fori_loop(1, n, go, 0)

    def finish(outgoing, incoming, sem):
        every = pltpu.make_async_remote_copy(
            src_ref=outgoing.at[pl.ds(0, n - 1)],
            dst_ref=incoming.at[pl.ds(0, n - 1)],
            send_sem=send_sems.at[sem],
            recv_sem=recv_sems.at[sem],
            device_id=(peer_of(me, 1),),
            device_id_type=MESH,
        )
        every.wait_recv()
        every.wait_send()

    send(asked, heard, 0)
    heard[me] = asked[me]
    finish(asked, heard, 0)
    diagonal = lax.broadcasted_iota(jnp.int32, heard.shape, 0) == lax.broadcasted_iota(
        jnp.int32, heard.shape, 2
    )
    row_ids[...] = jnp.sum(jnp.where(diagonal, heard[...], 0), axis=0)
    to_scalars = pltpu.make_async_copy(row_ids, ids, local_sem)
    to_scalars.start()
    to_scalars.wait()

    def pick_features(p, _):
        send_feat[p] = masked[jnp.maximum(ids[0, p], 0)]
        return 0

    lax.fori_loop(0, n, pick_features, 0)
    send(send_feat, got_feat, 1)

    def place_block(c, k, block):
        columns = slice(k * points, (k + 1) * points)
        for i in range(3):
            yaug[c, i * channels : (i + 1) * channels, columns] = block
        wide = block.astype(jnp.float32)
        norm = (-0.5 * UNIT) * jnp.sum(wide * wide, axis=0, keepdims=True)
        ynorm[c, :, columns] = norm
        yaug[c, top : top + AUX, columns] = aux_rows(3, norm, points)

    def own_block(c, _):
        place_block(c, 0, masked[c])
        return 0

    lax.fori_loop(0, cells, own_block, 0)
    finish(send_feat, got_feat, 1)

    for iteration in range(ITERS):

        def cell(c, carry):
            own, source = carry
            remote = [lax.shift_right_logical(near[c, k], 4) for k in range(LIST - 1)]
            if iteration == 0:
                for k in range(1, LIST):
                    place_block(c, k, got_feat[remote[k - 1]])
            else:
                xaug[c, top : top + AUX] = aux_rows(0, xnorm[c], points)
                for k in range(LIST):
                    columns = slice(k * points, (k + 1) * points)
                    held = pots[c] if k == 0 else got_pot[remote[k - 1]]
                    yaug[c, top : top + AUX, columns] = aux_rows(
                        3, ynorm[c, :, columns] + held, points
                    )
            peak = None
            for k in range(LIST):
                columns = slice(k * points, (k + 1) * points)
                block = cross(yaug[c, :, columns], xaug[c])
                scores[columns] = block
                here = jnp.max(block, axis=0, keepdims=True)
                peak = here if peak is None else jnp.maximum(peak, here)
            total = jnp.zeros((1, points), jnp.float32)
            for k in range(LIST):
                columns = slice(k * points, (k + 1) * points)
                total = total + jnp.sum(jnp.exp2(scores[columns] - peak), axis=0, keepdims=True)
            pot = jnp.where(lanes < src_len[c], -damping * (peak + jnp.log2(total)), 0.0)
            source = jnp.where(cell_row == c, pot, source)
            weight = jnp.where(lanes < src_len[c], pot + xnorm[c], NEVER)
            xaug[c, top : top + AUX] = aux_rows(0, weight, points)
            for k in range(LIST):
                columns = slice(k * points, (k + 1) * points)
                block = cross(xaug[c], yaug[c, :, columns])
                here = jnp.max(block, axis=0, keepdims=True)
                summed = jnp.sum(jnp.exp2(block - here), axis=0, keepdims=True)
                term = here + jnp.log2(summed)
                if iteration > 0:
                    held = pots[c] if k == 0 else got_pot[remote[k - 1]]
                    term = term - held
                if k == 0:
                    own = jnp.where(cell_row == c, term, own)
                else:
                    part[c * (LIST - 1) + k - 1] = term
            return own, source

        nothing = jnp.zeros((cells, points), jnp.float32)
        own, source = lax.fori_loop(0, cells, cell, (nothing, nothing))

        def pick_parts(p, _):
            send_part[iteration, p] = part[entry_of[p]]
            return 0

        lax.fori_loop(0, n, pick_parts, 0)
        send(send_part.at[iteration], got_part.at[iteration], 2 + 2 * iteration)
        if iteration == ITERS - 1:
            source_out[...] = source * (1.0 / UNIT)
        finish(send_part.at[iteration], got_part.at[iteration], 2 + 2 * iteration)

        def larger(p, largest):
            wins = jnp.maximum(largest, got_part[iteration, p])
            return jnp.where(cell_row == ids[0, p], wins, largest)

        largest = lax.fori_loop(0, n, larger, own)

        def add_up(p, totals):
            term = jnp.exp2(got_part[iteration, p] - largest)
            return totals + jnp.where(cell_row == ids[0, p], term, 0.0)

        totals = lax.fori_loop(0, n, add_up, jnp.exp2(own - largest))
        lengths = jnp.zeros((cells, points), jnp.int32)
        for c in range(cells):
            lengths = jnp.where(cell_row == c, tgt_len[c], lengths)
        live = lax.broadcasted_iota(jnp.int32, (cells, points), 1) < lengths
        target = jnp.where(live, -damping * (largest + jnp.log2(totals)), 0.0)
        if iteration == ITERS - 1:
            target_out[...] = target * (1.0 / UNIT)
        else:
            for c in range(cells):
                pots[c] = target[c : c + 1]

            def pick_pots(p, _):
                send_pot[p] = pots[jnp.maximum(ids[0, p], 0)]
                return 0

            lax.fori_loop(0, n, pick_pots, 0)
            send(send_pot, got_pot, 3)
            finish(send_pot, got_pot, 3)


def local(src_feat, tgt_feat, src_len, tgt_len, neighbours):
    cells, channels, points = src_feat.shape
    n = lax.axis_size("cells")
    wanted = neighbours.reshape(-1)
    hits = (wanted // cells)[None, :] == jnp.arange(n, dtype=jnp.int32)[:, None]
    entries = jnp.arange(wanted.shape[0], dtype=jnp.int32)[None, :]
    entry_of = jnp.max(jnp.where(hits, entries, 0), axis=1)
    asked = jnp.max(jnp.where(hits, (wanted % cells)[None, :], -1), axis=1)
    asked = jnp.broadcast_to(asked[:, None, None], (n, 1, 128))
    vmem = pl.BlockSpec(memory_space=pltpu.VMEM)
    smem = pl.BlockSpec(memory_space=pltpu.SMEM)
    deep = 3 * channels + AUX
    f32, bf16 = jnp.float32, jnp.bfloat16
    return pl.pallas_call(
        functools.partial(kernel, n),
        name="sinkhorn",
        out_shape=(jax.ShapeDtypeStruct((cells, points), f32),) * 2,
        in_specs=[vmem, vmem, smem, smem, smem, smem, vmem],
        out_specs=(vmem, vmem),
        scratch_shapes=[
            pltpu.VMEM((cells, channels, points), bf16),
            pltpu.VMEM((n, 1, 128), jnp.int32),
            pltpu.VMEM((1, 128), jnp.int32),
            pltpu.SMEM((1, 128), jnp.int32),
            pltpu.VMEM((n, channels, points), bf16),
            pltpu.VMEM((n, channels, points), bf16),
            pltpu.VMEM((cells, deep, points), bf16),
            pltpu.VMEM((cells, 1, points), f32),
            pltpu.VMEM((cells, deep, LIST * points), bf16),
            pltpu.VMEM((cells, 1, LIST * points), f32),
            pltpu.VMEM((LIST * points, points), f32),
            pltpu.VMEM((cells * (LIST - 1), 1, points), f32),
            pltpu.VMEM((cells, 1, points), f32),
            pltpu.VMEM((ITERS, n, 1, points), f32),
            pltpu.VMEM((ITERS, n, 1, points), f32),
            pltpu.VMEM((n, 1, points), f32),
            pltpu.VMEM((n, 1, points), f32),
            pltpu.SemaphoreType.DMA((5,)),
            pltpu.SemaphoreType.DMA((5,)),
            pltpu.SemaphoreType.DMA(()),
        ],
        compiler_params=pltpu.CompilerParams(
            collective_id=0, has_side_effects=True, vmem_limit_bytes=56 * 2**20
        ),
    )(src_feat, tgt_feat, src_len, tgt_len, neighbours, entry_of, asked)


def solution(mesh):
    split = P("cells")
    return jax.shard_map(
        local,
        mesh=mesh,
        in_specs=(split,) * 5,
        out_specs=(split, split),
        check_vma=False,
    )
```

time: 262 us -> 139 us (0.53)
  Pallas kernels: 0 us -> 134 us
  blocking collectives: 64.6 us -> 0 us
  other arithmetic: 54.1 us -> 0.63 us
  local copies, waits for them, and re-layouts: 45.8 us -> 3.61 us
  matrix products: 41.3 us -> 0 us
  waiting for transfers between devices: 30.6 us -> 0 us
  starting transfers between devices: 17.8 us -> 0 us
  loops' own time: 5 us -> 0 us
    pallas_call x0 -> x1, Pallas kernels: none -> 134 us  [local(): pl.pallas_call(functools.partial(kernel, n), name='sinkhorn', out_shape=(...]
    dot_general x66 -> x0, matrix products: 41.3 us -> none  [the longest x64 40.1 us: pair_costs(): jnp.einsum('gfp,gkfq->gpkq', source_block, target_block, preferred_elemen...]
    unnamed x1 -> x0, blocking collectives: 37.3 us -> none
    all_to_all x4 -> x0, waiting for transfers between devices: 30.6 us -> none  [the longest x2 21.1 us: side_by_side(): lax.all_to_all(both, axis, split_axis=split_dim, concat_axis=concat_dim,...]
    dynamic_slice x128 -> x0, local copies, waits for them, and re-layouts: 21.5 us -> none  [in_groups(): result = lax.map(lambda items: function(*items), shaped)]
    eq x32 -> x0, other arithmetic: 21.5 us -> none  [largest_of(): hits = incoming_ids[:, None] == cell_group[None, :]]
    all_to_all x1 -> x0, blocking collectives: 20.8 us -> none  [local(): lax.all_to_all(outgoing.reshape(devices, per_owner), CELLS, split_axis=0,...]
    all_to_all x4 -> x0, starting transfers between devices: 17.8 us -> none  [the longest x2 8.44 us: side_by_side(): lax.all_to_all(both, axis, split_axis=split_dim, concat_axis=concat_dim,...]
  transfers between devices with their start and end apart: 4 -> 0, of which waited for: 3 -> 0; matrix products, arithmetic and copies ran while one was open for 1% -> 0% of each run, Pallas kernels for 0% -> 0%
where the time goes in v1:
time: 139 us
  Pallas kernels  134 us (96%)
  local copies, waits for them, and re-layouts  3.61 us (3%)
    pallas_call x1, Pallas kernels, local(): pl.pallas_call(functools.partial(kernel, n), name='sinkhorn', out_shape=(...  134 us

profile of v1, /device:TPU:1, one launch (start us, length us, event | category | flops | bytes accessed | tf_op | source)
XLA Modules:
  0.0 139.2 jit_solution(13315333931834137863)
XLA Ops:
  0.6 0.8 copy.12.near
  1.4 0.0 copy-start
  1.4 0.1 reshape.59
  1.5 0.6 select_reduce_fusion
  2.1 0.0 copy-done
  2.1 0.8 broadcast_in_dim.34.asked
  2.9 134.4 %sinkhorn.1 = (f32[16,256]{1,0:T(8,128)}, f32[16,256]{1,0:T(8,128)}) custom-call(bf16[16,32,256]{2,1,0:T(8,128)(2,1)} %src.1, bf16[16,32,256]{2,1,0:T(8,128)(2,1)} %tgt.1, s32[16]{0:T(128)} %src_len.1, s32[16]{0:T(128)} %tgt_len.1, s32[16,5]{1,0:T(8,128)} %copy-done, s32[128]{0:T(128)} %get-tuple-element.3.entry_of, s32[128,1,128]{2,1,0:T(1,128)} %broadcast_in_dim.34.asked), custom_call_target="tpu_custom_call" | custom-call | tf_op jit(solution)/shard_map/sinkhorn/pallas_call | solution.py:272
  137.3 0.0 copy-start.1
  137.3 1.3 copy.15
  138.6 0.0 copy-done.1
  138.6 0.6 copy.16
  (1 shorter events, 0.0 us)
Async XLA Ops:
  1.4 0.7 copy-start
  137.3 1.3 copy-start.1

commit v2 on v1

--- a/solution.py
+++ b/solution.py
@@ -20,10 +20,21 @@
 AUX = 16
 
 
-def peer_of(me, k):
-    core, y, z, x = me % 2, (me // 2) % 4, (me // 8) % 4, me // 32
-    dcore, dy, dz, dx = k % 2, (k // 2) % 4, (k // 8) % 4, k // 32
-    return ((((x + dx) % 4) * 4 + (z + dz) % 4) * 4 + (y + dy) % 4) * 2 + (core + dcore) % 2
+def each_peer(me, act):
+    core, y = lax.rem(me, 2), lax.rem(lax.div(me, 2), 4)
+    z, x = lax.rem(lax.div(me, 8), 4), lax.div(me, 32)
+    near = [lax.rem(y + dy, 4) * 2 + lax.rem(core + dc, 2) for dy in range(4) for dc in range(2)]
+    for j in range(1, 8):
+        act(x * 32 + z * 8 + near[j])
+
+    def plane(i, _):
+        k = lax.rem(i * 7, 16)
+        base = lax.rem(x + lax.div(k, 4), 4) * 32 + lax.rem(z + lax.rem(k, 4), 4) * 8
+        for j in range(8):
+            act(base + near[j])
+        return 0
+
+    lax.fori_loop(1, 16, plane, 0)
 
 
 def three_parts(value):
@@ -85,11 +96,10 @@
 
     barrier = pltpu.get_barrier_semaphore()
 
-    def greet(k, _):
-        pl.semaphore_signal(barrier, inc=1, device_id=(peer_of(me, k),), device_id_type=MESH)
-        return 0
-
-    lax.fori_loop(1, n, greet, 0)
+    def greet(peer):
+        pl.semaphore_signal(barrier, inc=1, device_id=(peer,), device_id_type=MESH)
+
+    each_peer(me, greet)
 
     def prepare(c, _):
         live = lanes < tgt_len[c]
@@ -106,8 +116,7 @@
     pl.semaphore_wait(barrier, n - 1)
 
     def send(outgoing, incoming, sem):
-        def go(k, _):
-            peer = peer_of(me, k)
+        def go(peer):
             pltpu.make_async_remote_copy(
                 src_ref=outgoing.at[peer],
                 dst_ref=incoming.at[me],
@@ -116,9 +125,8 @@
                 device_id=(peer,),
                 device_id_type=MESH,
             ).start()
-            return 0
-
-        lax.fori_loop(1, n, go, 0)
+
+        each_peer(me, go)
 
     def finish(outgoing, incoming, sem):
         every = pltpu.make_async_remote_copy(
@@ -126,7 +134,7 @@
             dst_ref=incoming.at[pl.ds(0, n - 1)],
             send_sem=send_sems.at[sem],
             recv_sem=recv_sems.at[sem],
-            device_id=(peer_of(me, 1),),
+            device_id=(lax.rem(me + 1, n),),
             device_id_type=MESH,
         )
         every.wait_recv()
@@ -147,7 +155,7 @@
         send_feat[p] = masked[jnp.maximum(ids[0, p], 0)]
         return 0
 
-    lax.fori_loop(0, n, pick_features, 0)
+    lax.fori_loop(0, n, pick_features, 0, unroll=8)
     send(send_feat, got_feat, 1)
 
     def place_block(c, k, block):
@@ -219,7 +227,7 @@
             send_part[iteration, p] = part[entry_of[p]]
             return 0
 
-        lax.fori_loop(0, n, pick_parts, 0)
+        lax.fori_loop(0, n, pick_parts, 0, unroll=8)
         send(send_part.at[iteration], got_part.at[iteration], 2 + 2 * iteration)
         if iteration == ITERS - 1:
             source_out[...] = source * (1.0 / UNIT)
@@ -229,13 +237,13 @@
             wins = jnp.maximum(largest, got_part[iteration, p])
             return jnp.where(cell_row == ids[0, p], wins, largest)
 
-        largest = lax.fori_loop(0, n, larger, own)
+        largest = lax.fori_loop(0, n, larger, own, unroll=8)
 
         def add_up(p, totals):
             term = jnp.exp2(got_part[iteration, p] - largest)
             return totals + jnp.where(cell_row == ids[0, p], term, 0.0)
 
-        totals = lax.fori_loop(0, n, add_up, jnp.exp2(own - largest))
+        totals = lax.fori_loop(0, n, add_up, jnp.exp2(own - largest), unroll=8)
         lengths = jnp.zeros((cells, points), jnp.int32)
         for c in range(cells):
             lengths = jnp.where(cell_row == c, tgt_len[c], lengths)
@@ -251,7 +259,7 @@
                 send_pot[p] = pots[jnp.maximum(ids[0, p], 0)]
                 return 0
 
-            lax.fori_loop(0, n, pick_pots, 0)
+            lax.fori_loop(0, n, pick_pots, 0, unroll=8)
             send(send_pot, got_pot, 3)
             finish(send_pot, got_pot, 3)
 

time: 139 us -> 112 us (0.81)
  Pallas kernels: 134 us -> 107 us
    pallas_call x1, Pallas kernels: 134 us -> 107 us  [local(): pl.pallas_call(functools.partial(kernel, n), name='sinkhorn', out_shape=(...]
where the time goes in v2:
time: 112 us
  Pallas kernels  107 us (96%)
  local copies, waits for them, and re-layouts  3.61 us (3%)
    pallas_call x1, Pallas kernels, local(): pl.pallas_call(functools.partial(kernel, n), name='sinkhorn', out_shape=(...  107 us
    unnamed x7, local copies, waits for them, and re-layouts  2.71 us

profile of v2, /device:TPU:1, one launch (start us, length us, event | category | flops | bytes accessed | tf_op | source)
XLA Modules:
  0.0 111.7 jit_solution(11241420538356763563)
XLA Ops:
  0.6 0.8 copy.12.near
  1.4 0.0 copy-start
  1.4 0.1 reshape.59
  1.5 0.6 select_reduce_fusion
  2.1 0.0 copy-done
  2.1 0.8 broadcast_in_dim.34.asked
  2.9 106.8 %sinkhorn.1 = (f32[16,256]{1,0:T(8,128)}, f32[16,256]{1,0:T(8,128)}) custom-call(bf16[16,32,256]{2,1,0:T(8,128)(2,1)} %src.1, bf16[16,32,256]{2,1,0:T(8,128)(2,1)} %tgt.1, s32[16]{0:T(128)} %src_len.1, s32[16]{0:T(128)} %tgt_len.1, s32[16,5]{1,0:T(8,128)} %copy-done, s32[128]{0:T(128)} %get-tuple-element.3.entry_of, s32[128,1,128]{2,1,0:T(1,128)} %broadcast_in_dim.34.asked), custom_call_target="tpu_custom_call" | custom-call | tf_op jit(solution)/shard_map/sinkhorn/pallas_call | solution.py:280
  109.7 0.0 copy-start.1
  109.7 1.3 %copy.15 = f32[16,256]{1,0:T(8,128)} copy(f32[16,256]{1,0:T(8,128)} %get-tuple-element.8) | data formatting | bytes 32768
  111.0 0.0 copy-done.1
  111.0 0.6 copy.16
  (1 shorter events, 0.0 us)
Async XLA Ops:
  1.4 0.7 copy-start
  109.7 1.3 %copy-start.1 = (f32[16,256]{1,0:T(8,128)S(1)}, f32[16,256]{1,0:T(8,128)}, u32[]{:S(2)}) copy-start(f32[16,256]{1,0:T(8,128)} %get-tuple-element.9) | copy-start | bytes 49156

commit v3 on v2

v3 whole, which is shorter than its diff:
```python
import functools
import math

import jax
import jax.numpy as jnp
from jax import lax
from jax.experimental import pallas as pl
from jax.experimental.pallas import tpu as pltpu
from jax.sharding import PartitionSpec as P

MESH = pl.DeviceIdType.MESH
ITERS = 2
LIST = 6
entropy_scale = 0.5
marginal_weight = 1.0
damping = marginal_weight / (marginal_weight + entropy_scale)
UNIT = math.log2(math.e) / entropy_scale
NEVER = -1.0e30
FAR = 2.0**50
AUX = 16


def coordinates(me):
    return lax.div(me, 32), lax.rem(lax.div(me, 8), 4), lax.rem(lax.div(me, 2), 4), lax.rem(me, 2)


def plane_of(x, z, i, sign):
    k = lax.rem(i * 7, 16)
    dx, dz = lax.div(k, 4), lax.rem(k, 4)
    if sign < 0:
        dx, dz = 4 - dx, 4 - dz
    return lax.rem(x + dx, 4) * 32 + lax.rem(z + dz, 4) * 8


def each_peer(me, act):
    x, z, y, core = coordinates(me)
    near = [lax.rem(y + dy, 4) * 2 + lax.rem(core + dc, 2) for dy in range(4) for dc in range(2)]
    for j in range(1, 8):
        act(x * 32 + z * 8 + near[j], 0)

    def plane(i, _):
        base = plane_of(x, z, i, 1)
        for j in range(8):
            act(base + near[j], i)
        return 0

    lax.fori_loop(1, 16, plane, 0)


def three_parts(value):
    high = value.astype(jnp.bfloat16).astype(jnp.float32)
    rest = value - high
    middle = rest.astype(jnp.bfloat16).astype(jnp.float32)
    return high, middle, rest - middle


def aux_rows(first, value, points):
    row = lax.broadcasted_iota(jnp.int32, (AUX, points), 0)
    rows = jnp.where(row < 6, 1.0, 0.0)
    for i, piece in enumerate(three_parts(value)):
        rows = jnp.where(row == first + i, piece, rows)
    return rows.astype(jnp.bfloat16)


def cross(a, b):
    return lax.dot_general(a, b, (((0,), (0,)), ((), ())), preferred_element_type=jnp.float32)


def column_lse(a, b):
    half = b.shape[1] // 2
    terms = []
    for columns in (slice(0, half), slice(half, 2 * half)):
        block = cross(a, b[:, columns])
        peak = jnp.max(block, axis=0, keepdims=True)
        terms.append(peak + jnp.log2(jnp.sum(jnp.exp2(block - peak), axis=0, keepdims=True)))
    return jnp.concatenate(terms, axis=1)


def kernel(
    n,
    src,
    tgt,
    src_len,
    tgt_len,
    near,
    entry_of,
    asked,
    source_out,
    target_out,
    masked,
    heard,
    row_ids,
    ids,
    send_feat,
    got_feat,
    xaug,
    xnorm,
    yown,
    yown_norm,
    yslot,
    yslot_norm,
    lse_own,
    lse_slot,
    part,
    pots,
    send_part,
    got_part,
    send_pot,
    got_pot,
    send_sems,
    recv_sems,
    feat_sems,
    local_sem,
):
    cells, channels, points = src.shape
    me = lax.axis_index("cells")
    lanes = lax.broadcasted_iota(jnp.int32, (1, points), 1)
    cell_row = lax.broadcasted_iota(jnp.int32, (cells, points), 0)
    top = 3 * channels

    barrier = pltpu.get_barrier_semaphore()

    def greet(peer, _):
        pl.semaphore_signal(barrier, inc=1, device_id=(peer,), device_id_type=MESH)

    each_peer(me, greet)

    def prepare(c, _):
        live = lanes < tgt_len[c]
        masked[c] = jnp.where(live, tgt[c].astype(jnp.float32), FAR).astype(jnp.bfloat16)
        x = src[c].astype(jnp.float32)
        for i, piece in enumerate(three_parts(x * UNIT)):
            xaug[c, i * channels : (i + 1) * channels] = piece.astype(jnp.bfloat16)
        norm = (-0.5 * UNIT) * jnp.sum(x * x, axis=0, keepdims=True)
        xnorm[c] = norm
        xaug[c, top : top + AUX] = aux_rows(0, norm, points)
        return 0

    lax.fori_loop(0, cells, prepare, 0, unroll=2)
    pl.semaphore_wait(barrier, n - 1)

    def send(outgoing, incoming, sem):
        def go(peer, _):
            pltpu.make_async_remote_copy(
                src_ref=outgoing.at[peer],
                dst_ref=incoming.at[me],
                send_sem=send_sems.at[sem],
                recv_sem=recv_sems.at[sem],
                device_id=(peer,),
                device_id_type=MESH,
            ).start()

        each_peer(me, go)

    def arrival(outgoing, incoming, first, count, send_sem, recv_sem):
        return pltpu.make_async_remote_copy(
            src_ref=outgoing.at[pl.ds(0, count)],
            dst_ref=incoming.at[pl.ds(first, count)],
            send_sem=send_sem,
            recv_sem=recv_sem,
            device_id=(lax.rem(me + 1, n),),
            device_id_type=MESH,
        )

    def finish(outgoing, incoming, sem):
        every = arrival(outgoing, incoming, 0, n - 1, send_sems.at[sem], recv_sems.at[sem])
        every.wait_recv()
        every.wait_send()

    send(asked, heard, 0)
    heard[me] = asked[me]
    finish(asked, heard, 0)
    diagonal = lax.broadcasted_iota(jnp.int32, heard.shape, 0) == lax.broadcasted_iota(
        jnp.int32, heard.shape, 2
    )
    row_ids[...] = jnp.sum(jnp.where(diagonal, heard[...], 0), axis=0)
    to_scalars = pltpu.make_async_copy(row_ids, ids, local_sem)
    to_scalars.start()
    to_scalars.wait()

    def pick_features(p, _):
        send_feat[p] = masked[jnp.maximum(ids[0, p], 0)]
        return 0

    lax.fori_loop(0, n, pick_features, 0, unroll=8)

    def send_features(peer, i):
        pltpu.make_async_remote_copy(
            src_ref=send_feat.at[peer],
            dst_ref=got_feat.at[me],
            send_sem=send_sems.at[1],
            recv_sem=feat_sems.at[i],
            device_id=(peer,),
            device_id_type=MESH,
        ).start()

    each_peer(me, send_features)
    got_feat[me] = masked[0]

    def place(block, spread, norms, at):
        for i in range(3):
            spread[at, i * channels : (i + 1) * channels] = block
        wide = block.astype(jnp.float32)
        norm = (-0.5 * UNIT) * jnp.sum(wide * wide, axis=0, keepdims=True)
        norms[at] = norm
        spread[at, top : top + AUX] = aux_rows(3, norm, points)

    def first_own(g, _):
        for j in range(8):
            c = g * 8 + j
            place(masked[c], yown, yown_norm, c)
            lse_own[c] = column_lse(yown[c], xaug[c])
        return 0

    lax.fori_loop(0, cells // 8, first_own, 0)

    x, z, _, _ = coordinates(me)

    def first_slots(i, _):
        base = plane_of(x, z, i, -1)
        arrival(send_feat, got_feat, base, 8, send_sems.at[1], feat_sems.at[i]).wait_recv()
        slots(base)
        return 0

    def slots(base):
        for j in range(8):
            slot = base + j
            place(got_feat[slot], yslot, yslot_norm, slot)
            cell = lax.shift_right_logical(entry_of[slot], 3)
            lse_slot[slot] = column_lse(yslot[slot], xaug[cell])

    home = x * 32 + z * 8
    arrival(send_feat, got_feat, home, 7, send_sems.at[1], feat_sems.at[0]).wait_recv()
    slots(home)
    lax.fori_loop(1, 16, first_slots, 0)
    arrival(send_feat, got_feat, 0, n - 1, send_sems.at[1], feat_sems.at[0]).wait_send()

    def slot_of(c, k):
        return lax.shift_right_logical(near[c, k], 4)

    def stack(rows):
        return jnp.concatenate([rows[c] for c in range(cells)], axis=0)

    for iteration in range(ITERS):
        last = iteration == ITERS - 1

        if iteration > 0:

            def second_rows(g, _):
                for j in range(4):
                    c = g * 4 + j
                    for k in range(LIST - 1):
                        slot = slot_of(c, k)
                        aux = aux_rows(3, yslot_norm[slot] + got_pot[slot], points)
                        block = jnp.concatenate([yslot[slot][:top], aux], axis=0)
                        lse_slot[c * 8 + k] = column_lse(block, xaug[c])
                return 0

            lax.fori_loop(0, cells // 4, second_rows, 0)

        def source_update(c, _):
            if iteration == 0:
                terms = [lse_slot[slot_of(c, k)] for k in range(LIST - 1)] + [lse_own[c]]
            else:
                terms = [lse_slot[c * 8 + k] for k in range(LIST - 1)] + [lse_own[c]]
            peak = functools.reduce(jnp.maximum, terms)
            total = sum(jnp.exp2(term - peak) for term in terms)
            live = lanes < src_len[c]
            pot = jnp.where(live, -damping * (peak + jnp.log2(total)), 0.0)
            if last:
                pots[c] = pot
            xaug[c, top : top + AUX] = aux_rows(0, jnp.where(live, pot + xnorm[c], NEVER), points)
            return 0

        lax.fori_loop(0, cells, source_update, 0, unroll=8)

        def columns(g, _):
            for j in range(4):
                c = g * 4 + j
                for k in range(LIST - 1):
                    part[c * 8 + k] = column_lse(xaug[c], yslot[slot_of(c, k)])
            return 0

        lax.fori_loop(0, cells // 4, columns, 0)

        def pick_parts(p, _):
            send_part[iteration, p] = part[entry_of[p]]
            return 0

        lax.fori_loop(0, n, pick_parts, 0, unroll=8)
        send(send_part.at[iteration], got_part.at[iteration], 2 + 2 * iteration)

        def own_columns(g, _):
            for j in range(8):
                lse_own[g * 8 + j] = column_lse(xaug[g * 8 + j], yown[g * 8 + j])
            return 0

        lax.fori_loop(0, cells // 8, own_columns, 0)
        if last:
            source_out[...] = stack(pots) * (1.0 / UNIT)
        own = stack(lse_own)
        finish(send_part.at[iteration], got_part.at[iteration], 2 + 2 * iteration)

        def larger(p, largest):
            wins = jnp.maximum(largest, got_part[iteration, p])
            return jnp.where(cell_row == ids[0, p], wins, largest)

        largest = lax.fori_loop(0, n, larger, own, unroll=8)

        def add_up(p, totals):
            term = jnp.exp2(got_part[iteration, p] - largest)
            return totals + jnp.where(cell_row == ids[0, p], term, 0.0)

        totals = lax.fori_loop(0, n, add_up, jnp.exp2(own - largest), unroll=8)
        lengths = jnp.zeros((cells, points), jnp.int32)
        for c in range(cells):
            lengths = jnp.where(cell_row == c, tgt_len[c], lengths)
        live = lax.broadcasted_iota(jnp.int32, (cells, points), 1) < lengths
        target = jnp.where(live, -damping * (largest + jnp.log2(totals)), 0.0)
        if last:
            target_out[...] = target * (1.0 / UNIT)
        else:
            for c in range(cells):
                pots[c] = target[c : c + 1]

            def pick_pots(p, _):
                send_pot[p] = pots[jnp.maximum(ids[0, p], 0)]
                return 0

            lax.fori_loop(0, n, pick_pots, 0, unroll=8)
            send(send_pot, got_pot, 3)

            def own_rows(g, _):
                for j in range(8):
                    c = g * 8 + j
                    xaug[c, top : top + AUX] = aux_rows(0, xnorm[c], points)
                    aux = aux_rows(3, yown_norm[c] + pots[c], points)
                    block = jnp.concatenate([yown[c][:top], aux], axis=0)
                    lse_own[c] = column_lse(block, xaug[c])
                return 0

            lax.fori_loop(0, cells // 8, own_rows, 0)
            finish(send_pot, got_pot, 3)


def local(src_feat, tgt_feat, src_len, tgt_len, neighbours):
    cells, channels, points = src_feat.shape
    n = lax.axis_size("cells")
    wanted = neighbours.reshape(-1)
    hits = (wanted // cells)[None, :] == jnp.arange(n, dtype=jnp.int32)[:, None]
    order = jnp.arange(wanted.shape[0], dtype=jnp.int32)[None, :]
    entries = order // 5 * 8 + order % 5
    entry_of = jnp.max(jnp.where(hits, entries, 0), axis=1)
    asked = jnp.max(jnp.where(hits, (wanted % cells)[None, :], -1), axis=1)
    asked = jnp.broadcast_to(asked[:, None, None], (n, 1, 128))
    vmem = pl.BlockSpec(memory_space=pltpu.VMEM)
    smem = pl.BlockSpec(memory_space=pltpu.SMEM)
    deep = 3 * channels + AUX
    f32, bf16 = jnp.float32, jnp.bfloat16
    return pl.pallas_call(
        functools.partial(kernel, n),
        name="sinkhorn",
        out_shape=(jax.ShapeDtypeStruct((cells, points), f32),) * 2,
        in_specs=[vmem, vmem, smem, smem, smem, smem, vmem],
        out_specs=(vmem, vmem),
        scratch_shapes=[
            pltpu.VMEM((cells, channels, points), bf16),
            pltpu.VMEM((n, 1, 128), jnp.int32),
            pltpu.VMEM((1, 128), jnp.int32),
            pltpu.SMEM((1, 128), jnp.int32),
            pltpu.VMEM((n, channels, points), bf16),
            pltpu.VMEM((n, channels, points), bf16),
            pltpu.VMEM((cells, deep, points), bf16),
            pltpu.VMEM((cells, 1, points), f32),
            pltpu.VMEM((cells, deep, points), bf16),
            pltpu.VMEM((cells, 1, points), f32),
            pltpu.VMEM((n, deep, points), bf16),
            pltpu.VMEM((n, 1, points), f32),
            pltpu.VMEM((cells, 1, points), f32),
            pltpu.VMEM((n, 1, points), f32),
            pltpu.VMEM((cells * 8, 1, points), f32),
            pltpu.VMEM((cells, 1, points), f32),
            pltpu.VMEM((ITERS, n, 1, points), f32),
            pltpu.VMEM((ITERS, n, 1, points), f32),
            pltpu.VMEM((n, 1, points), f32),
            pltpu.VMEM((n, 1, points), f32),
            pltpu.SemaphoreType.DMA((5,)),
            pltpu.SemaphoreType.DMA((5,)),
            pltpu.SemaphoreType.DMA((16,)),
            pltpu.SemaphoreType.DMA(()),
        ],
        compiler_params=pltpu.CompilerParams(
            collective_id=0, has_side_effects=True, vmem_limit_bytes=56 * 2**20
        ),
    )(src_feat, tgt_feat, src_len, tgt_len, neighbours, entry_of, asked)


def solution(mesh):
    split = P("cells")
    return jax.shard_map(
        local,
        mesh=mesh,
        in_specs=(split,) * 5,
        out_specs=(split, split),
        check_vma=False,
    )
```

time: 112 us -> 93.7 us (0.84)
  Pallas kernels: 107 us -> 88.1 us
    pallas_call x1, Pallas kernels: 107 us -> 88.1 us  [local(): pl.pallas_call(functools.partial(kernel, n), name='sinkhorn', out_shape=(...]
where the time goes in v3:
time: 93.7 us; the launch traced here: 93.5 us
  Pallas kernels  88.1 us (94%)
  local copies, waits for them, and re-layouts  4.09 us (4%)
    pallas_call x1, Pallas kernels, local(): pl.pallas_call(functools.partial(kernel, n), name='sinkhorn', out_shape=(...  88.1 us
    unnamed x7, local copies, waits for them, and re-layouts  3.19 us

profile of v3, /device:TPU:1, one launch (start us, length us, event | category | flops | bytes accessed | tf_op | source)
XLA Modules:
  0.0 93.5 jit_solution(1703386673171560771)
XLA Ops:
  0.6 0.8 copy.12.near
  1.4 0.0 copy-start
  1.4 0.1 reshape.97
  1.5 0.5 copy-done
  2.0 0.6 select_reduce_fusion
  2.6 0.8 broadcast_in_dim.34.asked
  3.4 88.1 %sinkhorn.1 = (f32[16,256]{1,0:T(8,128)}, f32[16,256]{1,0:T(8,128)}) custom-call(bf16[16,32,256]{2,1,0:T(8,128)(2,1)} %src.1, bf16[16,32,256]{2,1,0:T(8,128)(2,1)} %tgt.1, s32[16]{0:T(128)} %src_len.1, s32[16]{0:T(128)} %tgt_len.1, s32[16,5]{1,0:T(8,128)} %copy-done, s32[128]{0:T(128)} %get-tuple-element.3.entry_of, s32[128,1,128]{2,1,0:T(1,128)} %broadcast_in_dim.34.asked), custom_call_target="tpu_custom_call" | custom-call | tf_op jit(solution)/shard_map/sinkhorn/pallas_call | solution.py:360
  91.6 0.0 copy-start.1
  91.6 1.3 %copy.15 = f32[16,256]{1,0:T(8,128)} copy(f32[16,256]{1,0:T(8,128)} %get-tuple-element.9) | data formatting | bytes 32768
  92.9 0.0 copy-done.1
  92.9 0.6 copy.16
  (1 shorter events, 0.0 us)
Async XLA Ops:
  1.4 0.6 copy-start
  91.6 1.3 %copy-start.1 = (f32[16,256]{1,0:T(8,128)S(1)}, f32[16,256]{1,0:T(8,128)}, u32[]{:S(2)}) copy-start(f32[16,256]{1,0:T(8,128)} %get-tuple-element.10) | copy-start | bytes 49156

commit v4 on v3

--- a/solution.py
+++ b/solution.py
@@ -24,27 +24,38 @@
     return lax.div(me, 32), lax.rem(lax.div(me, 8), 4), lax.rem(lax.div(me, 2), 4), lax.rem(me, 2)
 
 
-def plane_of(x, z, i, sign):
-    k = lax.rem(i * 7, 16)
-    dx, dz = lax.div(k, 4), lax.rem(k, 4)
+def plane_of(x, z, i, sign, far_first):
+    if far_first:
+        dx, dz = 6 - lax.div(i, 4), 6 - lax.rem(i, 4)
+    else:
+        k = lax.rem(i * 7, 16)
+        dx, dz = lax.div(k, 4), lax.rem(k, 4)
     if sign < 0:
         dx, dz = 4 - dx, 4 - dz
     return lax.rem(x + dx, 4) * 32 + lax.rem(z + dz, 4) * 8
 
 
-def each_peer(me, act):
+def each_peer(me, act, far_first=True):
     x, z, y, core = coordinates(me)
-    near = [lax.rem(y + dy, 4) * 2 + lax.rem(core + dc, 2) for dy in range(4) for dc in range(2)]
-    for j in range(1, 8):
-        act(x * 32 + z * 8 + near[j], 0)
+    near = [lax.rem(y + dy, 4) * 2 + lax.rem(core + dc, 2) for dy in (2, 1, 3, 0) for dc in range(2)]
 
     def plane(i, _):
-        base = plane_of(x, z, i, 1)
+        base = plane_of(x, z, i, 1, far_first)
         for j in range(8):
             act(base + near[j], i)
         return 0
 
-    lax.fori_loop(1, 16, plane, 0)
+    def home(i):
+        for j in (0, 1, 2, 3, 4, 5, 7):
+            act(x * 32 + z * 8 + near[j], i)
+
+    if far_first:
+        lax.fori_loop(0, 10, plane, 0)
+        lax.fori_loop(11, 16, plane, 0)
+        home(10)
+    else:
+        home(0)
+        lax.fori_loop(1, 16, plane, 0)
 
 
 def three_parts(value):
@@ -83,14 +94,14 @@
     src_len,
     tgt_len,
     near,
-    entry_of,
-    asked,
     source_out,
     target_out,
     masked,
+    asked,
     heard,
     row_ids,
     ids,
+    held,
     send_feat,
     got_feat,
     xaug,
@@ -137,6 +148,27 @@
         return 0
 
     lax.fori_loop(0, cells, prepare, 0, unroll=2)
+
+    device_row = lax.broadcasted_iota(jnp.int32, (n, 128), 0)
+    on_diagonal = device_row == lax.broadcasted_iota(jnp.int32, (n, 128), 1)
+
+    def ask(c, table):
+        for k in range(LIST - 1):
+            wanted = near[k, c]
+            entry = (c * 8 + k) * 16 + jnp.bitwise_and(wanted, 15)
+            table = jnp.where(device_row == lax.shift_right_logical(wanted, 4), entry, table)
+        return table
+
+    table = lax.fori_loop(0, cells, ask, jnp.full((n, 128), -1, jnp.int32))
+    asked[...] = table.reshape(n, 1, 128)
+
+    def to_scalars(diagonal_of, at):
+        row_ids[at] = jnp.sum(jnp.where(on_diagonal, diagonal_of, 0), axis=0, keepdims=True)
+        copy = pltpu.make_async_copy(row_ids.at[at], ids.at[at], local_sem)
+        copy.start()
+        copy.wait()
+
+    to_scalars(table, 0)
     pl.semaphore_wait(barrier, n - 1)
 
     def send(outgoing, incoming, sem):
@@ -170,16 +202,19 @@
     send(asked, heard, 0)
     heard[me] = asked[me]
     finish(asked, heard, 0)
-    diagonal = lax.broadcasted_iota(jnp.int32, heard.shape, 0) == lax.broadcasted_iota(
-        jnp.int32, heard.shape, 2
-    )
-    row_ids[...] = jnp.sum(jnp.where(diagonal, heard[...], 0), axis=0)
-    to_scalars = pltpu.make_async_copy(row_ids, ids, local_sem)
-    to_scalars.start()
-    to_scalars.wait()
+    to_scalars(heard[...].reshape(n, 128), 1)
+
+    def entry_of(p):
+        return lax.shift_right_logical(jnp.maximum(ids[0, 0, p], 0), 4)
+
+    def cell_for(p):
+        return jnp.bitwise_and(ids[1, 0, p], 15)
+
+    def row_for(p):
+        return jnp.where(ids[1, 0, p] < 0, -1, cell_for(p))
 
     def pick_features(p, _):
-        send_feat[p] = masked[jnp.maximum(ids[0, p], 0)]
+        send_feat[p] = masked[cell_for(p)]
         return 0
 
     lax.fori_loop(0, n, pick_features, 0, unroll=8)
@@ -194,7 +229,7 @@
             device_id_type=MESH,
         ).start()
 
-    each_peer(me, send_features)
+    each_peer(me, send_features, False)
     got_feat[me] = masked[0]
 
     def place(block, spread, norms, at):
@@ -217,7 +252,7 @@
     x, z, _, _ = coordinates(me)
 
     def first_slots(i, _):
-        base = plane_of(x, z, i, -1)
+        base = plane_of(x, z, i, -1, False)
         arrival(send_feat, got_feat, base, 8, send_sems.at[1], feat_sems.at[i]).wait_recv()
         slots(base)
         return 0
@@ -226,7 +261,7 @@
         for j in range(8):
             slot = base + j
             place(got_feat[slot], yslot, yslot_norm, slot)
-            cell = lax.shift_right_logical(entry_of[slot], 3)
+            cell = lax.shift_right_logical(entry_of(slot), 3)
             lse_slot[slot] = column_lse(yslot[slot], xaug[cell])
 
     home = x * 32 + z * 8
@@ -236,7 +271,7 @@
     arrival(send_feat, got_feat, 0, n - 1, send_sems.at[1], feat_sems.at[0]).wait_send()
 
     def slot_of(c, k):
-        return lax.shift_right_logical(near[c, k], 4)
+        return lax.shift_right_logical(near[k, c], 4)
 
     def stack(rows):
         return jnp.concatenate([rows[c] for c in range(cells)], axis=0)
@@ -284,7 +319,7 @@
         lax.fori_loop(0, cells // 4, columns, 0)
 
         def pick_parts(p, _):
-            send_part[iteration, p] = part[entry_of[p]]
+            send_part[iteration, p] = part[entry_of(p)]
             return 0
 
         lax.fori_loop(0, n, pick_parts, 0, unroll=8)
@@ -297,19 +332,22 @@
 
         lax.fori_loop(0, cells // 8, own_columns, 0)
         if last:
-            source_out[...] = stack(pots) * (1.0 / UNIT)
+            source_out[...] = stack(pots)
         own = stack(lse_own)
         finish(send_part.at[iteration], got_part.at[iteration], 2 + 2 * iteration)
 
         def larger(p, largest):
             wins = jnp.maximum(largest, got_part[iteration, p])
-            return jnp.where(cell_row == ids[0, p], wins, largest)
+            return jnp.where(cell_row == row_for(p), wins, largest)
 
         largest = lax.fori_loop(0, n, larger, own, unroll=8)
 
+        for c in range(cells):
+            held[c] = largest[c : c + 1]
+
         def add_up(p, totals):
-            term = jnp.exp2(got_part[iteration, p] - largest)
-            return totals + jnp.where(cell_row == ids[0, p], term, 0.0)
+            term = jnp.exp2(got_part[iteration, p] - held[cell_for(p)])
+            return totals + jnp.where(cell_row == row_for(p), term, 0.0)
 
         totals = lax.fori_loop(0, n, add_up, jnp.exp2(own - largest), unroll=8)
         lengths = jnp.zeros((cells, points), jnp.int32)
@@ -318,13 +356,13 @@
         live = lax.broadcasted_iota(jnp.int32, (cells, points), 1) < lengths
         target = jnp.where(live, -damping * (largest + jnp.log2(totals)), 0.0)
         if last:
-            target_out[...] = target * (1.0 / UNIT)
+            target_out[...] = target
         else:
             for c in range(cells):
                 pots[c] = target[c : c + 1]
 
             def pick_pots(p, _):
-                send_pot[p] = pots[jnp.maximum(ids[0, p], 0)]
+                send_pot[p] = pots[cell_for(p)]
                 return 0
 
             lax.fori_loop(0, n, pick_pots, 0, unroll=8)
@@ -346,28 +384,23 @@
 def local(src_feat, tgt_feat, src_len, tgt_len, neighbours):
     cells, channels, points = src_feat.shape
     n = lax.axis_size("cells")
-    wanted = neighbours.reshape(-1)
-    hits = (wanted // cells)[None, :] == jnp.arange(n, dtype=jnp.int32)[:, None]
-    order = jnp.arange(wanted.shape[0], dtype=jnp.int32)[None, :]
-    entries = order // 5 * 8 + order % 5
-    entry_of = jnp.max(jnp.where(hits, entries, 0), axis=1)
-    asked = jnp.max(jnp.where(hits, (wanted % cells)[None, :], -1), axis=1)
-    asked = jnp.broadcast_to(asked[:, None, None], (n, 1, 128))
     vmem = pl.BlockSpec(memory_space=pltpu.VMEM)
     smem = pl.BlockSpec(memory_space=pltpu.SMEM)
     deep = 3 * channels + AUX
     f32, bf16 = jnp.float32, jnp.bfloat16
-    return pl.pallas_call(
+    potentials = pl.pallas_call(
         functools.partial(kernel, n),
         name="sinkhorn",
         out_shape=(jax.ShapeDtypeStruct((cells, points), f32),) * 2,
-        in_specs=[vmem, vmem, smem, smem, smem, smem, vmem],
+        in_specs=[vmem, vmem, smem, smem, smem],
         out_specs=(vmem, vmem),
         scratch_shapes=[
             pltpu.VMEM((cells, channels, points), bf16),
             pltpu.VMEM((n, 1, 128), jnp.int32),
-            pltpu.VMEM((1, 128), jnp.int32),
-            pltpu.SMEM((1, 128), jnp.int32),
+            pltpu.VMEM((n, 1, 128), jnp.int32),
+            pltpu.VMEM((2, 1, 128), jnp.int32),
+            pltpu.SMEM((2, 1, 128), jnp.int32),
+            pltpu.VMEM((cells, 1, points), f32),
             pltpu.VMEM((n, channels, points), bf16),
             pltpu.VMEM((n, channels, points), bf16),
             pltpu.VMEM((cells, deep, points), bf16),
@@ -392,7 +425,8 @@
         compiler_params=pltpu.CompilerParams(
             collective_id=0, has_side_effects=True, vmem_limit_bytes=56 * 2**20
         ),
-    )(src_feat, tgt_feat, src_len, tgt_len, neighbours, entry_of, asked)
+    )(src_feat, tgt_feat, src_len, tgt_len, neighbours.T)
+    return tuple(potential * (1.0 / UNIT) for potential in potentials)
 
 
 def solution(mesh):

time: 93.7 us -> 88.2 us (0.941)
  local copies, waits for them, and re-layouts: 4.09 us -> 0 us
  Pallas kernels: 88.1 us -> 86 us
    unnamed x7 -> x0, local copies, waits for them, and re-layouts: 3.19 us -> none
    pallas_call x1, Pallas kernels: 88.1 us -> 86 us  [local(): pl.pallas_call(functools.partial(kernel, n), name='sinkhorn', out_shape=(...]
    mul x0 -> x1, other arithmetic: none -> 1.35 us  [local(): return tuple((potential * (1.0 / UNIT) for potential in potentials))]
where the time goes in v4:
time: 88.2 us; the launch traced here: 88 us
  Pallas kernels  86 us (98%)
  other arithmetic  1.35 us (2%)
    pallas_call x1, Pallas kernels, local(): pl.pallas_call(functools.partial(kernel, n), name='sinkhorn', out_shape=(...  86 us

profile of v4, /device:TPU:1, one launch (start us, length us, event | category | flops | bytes accessed | tf_op | source)
XLA Modules:
  0.0 88.0 jit_solution(18090342360789845056)
XLA Ops:
  0.6 86.0 %sinkhorn.1 = (f32[16,256]{1,0:T(8,128)}, f32[16,256]{1,0:T(8,128)}) custom-call(bf16[16,32,256]{2,1,0:T(8,128)(2,1)} %src.1, bf16[16,32,256]{2,1,0:T(8,128)(2,1)} %tgt.1, s32[16]{0:T(128)} %src_len.1, s32[16]{0:T(128)} %tgt_len.1, s32[5,16]{1,0:T(8,128)} %bitcast.1), custom_call_target="tpu_custom_call" | custom-call | tf_op jit(solution)/shard_map/sinkhorn/pallas_call | solution.py:391
  86.6 1.4 %broadcast_multiply_fusion = (f32[16,256]{1,0:T(8,128)}, f32[16,256]{1,0:T(8,128)}) fusion(f32[16,256]{1,0:T(8,128)} %get-tuple-element.5, f32[16,256]{1,0:T(8,128)} %get-tuple-element.4), kind=kLoop, calls=%fused_computation | loop fusion | flops 8192 | bytes 65536 | tf_op jit(solution)/shard_map/mul | solution.py:429

commit v5 on v4

--- a/solution.py
+++ b/solution.py
@@ -16,6 +16,7 @@
 damping = marginal_weight / (marginal_weight + entropy_scale)
 UNIT = math.log2(math.e) / entropy_scale
 NEVER = -1.0e30
+LOWEST = -3.0e38
 FAR = 2.0**50
 AUX = 16
 
@@ -101,7 +102,6 @@
     heard,
     row_ids,
     ids,
-    held,
     send_feat,
     got_feat,
     xaug,
@@ -147,7 +147,6 @@
         xaug[c, top : top + AUX] = aux_rows(0, norm, points)
         return 0
 
-    lax.fori_loop(0, cells, prepare, 0, unroll=2)
 
     device_row = lax.broadcasted_iota(jnp.int32, (n, 128), 0)
     on_diagonal = device_row == lax.broadcasted_iota(jnp.int32, (n, 128), 1)
@@ -168,7 +167,6 @@
         copy.start()
         copy.wait()
 
-    to_scalars(table, 0)
     pl.semaphore_wait(barrier, n - 1)
 
     def send(outgoing, incoming, sem):
@@ -200,6 +198,8 @@
         every.wait_send()
 
     send(asked, heard, 0)
+    lax.fori_loop(0, cells, prepare, 0, unroll=2)
+    to_scalars(table, 0)
     heard[me] = asked[me]
     finish(asked, heard, 0)
     to_scalars(heard[...].reshape(n, 128), 1)
@@ -210,8 +210,17 @@
     def cell_for(p):
         return jnp.bitwise_and(ids[1, 0, p], 15)
 
-    def row_for(p):
-        return jnp.where(ids[1, 0, p] < 0, -1, cell_for(p))
+    packed = heard[...].reshape(n, 128)
+    asker_cell = jnp.where(packed < 0, -1, jnp.bitwise_and(packed, 15))
+    lane_of = lax.broadcasted_iota(jnp.int32, (n, 128), 1)
+    to_cell = jnp.where(asker_cell == lane_of, 1.0, 0.0).astype(jnp.bfloat16)
+    in_parts = jnp.logical_and(asker_cell == jnp.bitwise_and(lane_of, 15), lane_of < 3 * cells)
+    from_parts = jnp.where(in_parts, 1.0, 0.0).astype(jnp.bfloat16)
+
+    def for_askers(rows):
+        parts = list(three_parts(rows)) + [jnp.zeros((128 - 3 * cells, points), jnp.float32)]
+        stacked = jnp.concatenate(parts, axis=0).astype(jnp.bfloat16)
+        return jnp.dot(from_parts, stacked, preferred_element_type=jnp.float32)
 
     def pick_features(p, _):
         send_feat[p] = masked[cell_for(p)]
@@ -282,8 +291,8 @@
         if iteration > 0:
 
             def second_rows(g, _):
-                for j in range(4):
-                    c = g * 4 + j
+                for j in range(8):
+                    c = g * 8 + j
                     for k in range(LIST - 1):
                         slot = slot_of(c, k)
                         aux = aux_rows(3, yslot_norm[slot] + got_pot[slot], points)
@@ -291,7 +300,7 @@
                         lse_slot[c * 8 + k] = column_lse(block, xaug[c])
                 return 0
 
-            lax.fori_loop(0, cells // 4, second_rows, 0)
+            lax.fori_loop(0, cells // 8, second_rows, 0)
 
         def source_update(c, _):
             if iteration == 0:
@@ -310,13 +319,13 @@
         lax.fori_loop(0, cells, source_update, 0, unroll=8)
 
         def columns(g, _):
-            for j in range(4):
-                c = g * 4 + j
+            for j in range(8):
+                c = g * 8 + j
                 for k in range(LIST - 1):
                     part[c * 8 + k] = column_lse(xaug[c], yslot[slot_of(c, k)])
             return 0
 
-        lax.fori_loop(0, cells // 4, columns, 0)
+        lax.fori_loop(0, cells // 8, columns, 0)
 
         def pick_parts(p, _):
             send_part[iteration, p] = part[entry_of(p)]
@@ -336,20 +345,16 @@
         own = stack(lse_own)
         finish(send_part.at[iteration], got_part.at[iteration], 2 + 2 * iteration)
 
-        def larger(p, largest):
-            wins = jnp.maximum(largest, got_part[iteration, p])
-            return jnp.where(cell_row == row_for(p), wins, largest)
-
-        largest = lax.fori_loop(0, n, larger, own, unroll=8)
-
-        for c in range(cells):
-            held[c] = largest[c : c + 1]
-
-        def add_up(p, totals):
-            term = jnp.exp2(got_part[iteration, p] - held[cell_for(p)])
-            return totals + jnp.where(cell_row == row_for(p), term, 0.0)
-
-        totals = lax.fori_loop(0, n, add_up, jnp.exp2(own - largest), unroll=8)
+        terms = got_part[iteration].reshape(n, points)
+        asker = jnp.concatenate([asker_cell] * (points // 128), axis=1)
+        best = [
+            jnp.max(jnp.where(asker == c, terms, LOWEST), axis=0, keepdims=True)
+            for c in range(cells)
+        ]
+        largest = jnp.maximum(own, jnp.concatenate(best, axis=0))
+        shifted = jnp.where(asker >= 0, jnp.exp2(terms - for_askers(largest)), 0.0)
+        arrived = sum(cross(to_cell, piece.astype(jnp.bfloat16)) for piece in three_parts(shifted))
+        totals = jnp.exp2(own - largest) + arrived[:cells]
         lengths = jnp.zeros((cells, points), jnp.int32)
         for c in range(cells):
             lengths = jnp.where(cell_row == c, tgt_len[c], lengths)
@@ -360,12 +365,7 @@
         else:
             for c in range(cells):
                 pots[c] = target[c : c + 1]
-
-            def pick_pots(p, _):
-                send_pot[p] = pots[cell_for(p)]
-                return 0
-
-            lax.fori_loop(0, n, pick_pots, 0, unroll=8)
+            send_pot[...] = for_askers(target).reshape(n, 1, points)
             send(send_pot, got_pot, 3)
 
             def own_rows(g, _):
@@ -400,7 +400,6 @@
             pltpu.VMEM((n, 1, 128), jnp.int32),
             pltpu.VMEM((2, 1, 128), jnp.int32),
             pltpu.SMEM((2, 1, 128), jnp.int32),
-            pltpu.VMEM((cells, 1, points), f32),
             pltpu.VMEM((n, channels, points), bf16),
             pltpu.VMEM((n, channels, points), bf16),
             pltpu.VMEM((cells, deep, points), bf16),

time: 88.2 us -> 86.2 us (0.977)
  Pallas kernels: 86 us -> 84 us
    pallas_call x1, Pallas kernels: 86 us -> 84 us  [local(): pl.pallas_call(functools.partial(kernel, n), name='sinkhorn', out_shape=(...]
where the time goes in v5:
time: 86.2 us; the launch traced here: 86 us
  Pallas kernels  84 us (97%)
  other arithmetic  1.35 us (2%)
    pallas_call x1, Pallas kernels, local(): pl.pallas_call(functools.partial(kernel, n), name='sinkhorn', out_shape=(...  84 us

profile of v5, /device:TPU:1, one launch (start us, length us, event | category | flops | bytes accessed | tf_op | source)
XLA Modules:
  0.0 86.0 jit_solution(15820554843291123762)
XLA Ops:
  0.6 84.0 %sinkhorn.1 = (f32[16,256]{1,0:T(8,128)}, f32[16,256]{1,0:T(8,128)}) custom-call(bf16[16,32,256]{2,1,0:T(8,128)(2,1)} %src.1, bf16[16,32,256]{2,1,0:T(8,128)(2,1)} %tgt.1, s32[16]{0:T(128)} %src_len.1, s32[16]{0:T(128)} %tgt_len.1, s32[5,16]{1,0:T(8,128)} %bitcast.1), custom_call_target="tpu_custom_call" | custom-call | tf_op jit(solution)/shard_map/sinkhorn/pallas_call | solution.py:391
  84.6 1.4 %broadcast_multiply_fusion = (f32[16,256]{1,0:T(8,128)}, f32[16,256]{1,0:T(8,128)}) fusion(f32[16,256]{1,0:T(8,128)} %get-tuple-element.5, f32[16,256]{1,0:T(8,128)} %get-tuple-element.4), kind=kLoop, calls=%fused_computation | loop fusion | flops 8192 | bytes 65536 | tf_op jit(solution)/shard_map/mul | solution.py:428

commit v6 on v5

--- a/solution.py
+++ b/solution.py
@@ -222,23 +222,35 @@
         stacked = jnp.concatenate(parts, axis=0).astype(jnp.bfloat16)
         return jnp.dot(from_parts, stacked, preferred_element_type=jnp.float32)
 
-    def pick_features(p, _):
-        send_feat[p] = masked[cell_for(p)]
+    x, z, y, core = coordinates(me)
+    near_here = [lax.rem(y + dy, 4) * 2 + lax.rem(core + dc, 2) for dy in (2, 1, 3, 0) for dc in range(2)]
+    home = x * 32 + z * 8
+
+    def pick_plane(base):
+        for j in range(8):
+            send_feat[base + j] = masked[cell_for(base + j)]
+
+    def send_plane(base, i, others):
+        for j in others:
+            pltpu.make_async_remote_copy(
+                src_ref=send_feat.at[base + near_here[j]],
+                dst_ref=got_feat.at[me],
+                send_sem=send_sems.at[1],
+                recv_sem=feat_sems.at[i],
+                device_id=(base + near_here[j],),
+                device_id_type=MESH,
+            ).start()
+
+    def pick_then_send(i, _):
+        pick_plane(plane_of(x, z, i, 1, False))
+        send_plane(plane_of(x, z, i - 1, 1, False), i - 1, range(8))
         return 0
 
-    lax.fori_loop(0, n, pick_features, 0, unroll=8)
-
-    def send_features(peer, i):
-        pltpu.make_async_remote_copy(
-            src_ref=send_feat.at[peer],
-            dst_ref=got_feat.at[me],
-            send_sem=send_sems.at[1],
-            recv_sem=feat_sems.at[i],
-            device_id=(peer,),
-            device_id_type=MESH,
-        ).start()
-
-    each_peer(me, send_features, False)
+    pick_plane(home)
+    pick_plane(plane_of(x, z, 1, 1, False))
+    send_plane(home, 0, (0, 1, 2, 3, 4, 5, 7))
+    lax.fori_loop(2, 16, pick_then_send, 0)
+    send_plane(plane_of(x, z, 15, 1, False), 15, range(8))
     got_feat[me] = masked[0]
 
     def place(block, spread, norms, at):
@@ -258,7 +270,6 @@
 
     lax.fori_loop(0, cells // 8, first_own, 0)
 
-    x, z, _, _ = coordinates(me)
 
     def first_slots(i, _):
         base = plane_of(x, z, i, -1, False)
@@ -273,7 +284,6 @@
             cell = lax.shift_right_logical(entry_of(slot), 3)
             lse_slot[slot] = column_lse(yslot[slot], xaug[cell])
 
-    home = x * 32 + z * 8
     arrival(send_feat, got_feat, home, 7, send_sems.at[1], feat_sems.at[0]).wait_recv()
     slots(home)
     lax.fori_loop(1, 16, first_slots, 0)

time: 86.2 us -> 86.9 us (level)
  no operation moved by 1% of the time
where the time goes in v6:
time: 86.9 us; the launch traced here: 86.8 us
  Pallas kernels  84.8 us (98%)
  other arithmetic  1.35 us (2%)
    pallas_call x1, Pallas kernels, local(): pl.pallas_call(functools.partial(kernel, n), name='sinkhorn', out_shape=(...  84.8 us

profile of v6, /device:TPU:1, one launch (start us, length us, event | category | flops | bytes accessed | tf_op | source)
XLA Modules:
  0.0 86.8 jit_solution(14890444916880055136)
XLA Ops:
  0.6 84.8 %sinkhorn.1 = (f32[16,256]{1,0:T(8,128)}, f32[16,256]{1,0:T(8,128)}) custom-call(bf16[16,32,256]{2,1,0:T(8,128)(2,1)} %src.1, bf16[16,32,256]{2,1,0:T(8,128)(2,1)} %tgt.1, s32[16]{0:T(128)} %src_len.1, s32[16]{0:T(128)} %tgt_len.1, s32[5,16]{1,0:T(8,128)} %bitcast.1), custom_call_target="tpu_custom_call" | custom-call | tf_op jit(solution)/shard_map/sinkhorn/pallas_call | solution.py:401
  85.4 1.4 %broadcast_multiply_fusion = (f32[16,256]{1,0:T(8,128)}, f32[16,256]{1,0:T(8,128)}) fusion(f32[16,256]{1,0:T(8,128)} %get-tuple-element.5, f32[16,256]{1,0:T(8,128)} %get-tuple-element.4), kind=kLoop, calls=%fused_computation | loop fusion | flops 8192 | bytes 65536 | tf_op jit(solution)/shard_map/mul | solution.py:438

commit v7 on v5

--- a/solution.py
+++ b/solution.py
@@ -29,7 +29,7 @@
     if far_first:
         dx, dz = 6 - lax.div(i, 4), 6 - lax.rem(i, 4)
     else:
-        k = lax.rem(i * 7, 16)
+        k = lax.rem(i * 5, 16)
         dx, dz = lax.div(k, 4), lax.rem(k, 4)
     if sign < 0:
         dx, dz = 4 - dx, 4 - dz

time: 86.2 us -> 86 us (level)
  no operation moved by 1% of the time
where the time goes in v7:
time: 86 us; the launch traced here: 85.9 us
  Pallas kernels  84 us (98%)
  other arithmetic  1.35 us (2%)
    pallas_call x1, Pallas kernels, local(): pl.pallas_call(functools.partial(kernel, n), name='sinkhorn', out_shape=(...  84 us

profile of v7, /device:TPU:1, one launch (start us, length us, event | category | flops | bytes accessed | tf_op | source)
XLA Modules:
  0.0 85.9 jit_solution(10360673518707109764)
XLA Ops:
  0.6 84.0 %sinkhorn.1 = (f32[16,256]{1,0:T(8,128)}, f32[16,256]{1,0:T(8,128)}) custom-call(bf16[16,32,256]{2,1,0:T(8,128)(2,1)} %src.1, bf16[16,32,256]{2,1,0:T(8,128)(2,1)} %tgt.1, s32[16]{0:T(128)} %src_len.1, s32[16]{0:T(128)} %tgt_len.1, s32[5,16]{1,0:T(8,128)} %bitcast.1), custom_call_target="tpu_custom_call" | custom-call | tf_op jit(solution)/shard_map/sinkhorn/pallas_call | solution.py:391
  84.6 1.4 %broadcast_multiply_fusion = (f32[16,256]{1,0:T(8,128)}, f32[16,256]{1,0:T(8,128)}) fusion(f32[16,256]{1,0:T(8,128)} %get-tuple-element.5, f32[16,256]{1,0:T(8,128)} %get-tuple-element.4), kind=kLoop, calls=%fused_computation | loop fusion | flops 8192 | bytes 65536 | tf_op jit(solution)/shard_map/mul | solution.py:428
